TPU v7x, 32 devices: a whole 2x2x4 slice. The times are simulated.
32 devices in a mesh: blk: 16 (over z, y, core), rep: 2 (over x).
Axes of the slice: x: 2, y: 2, z: 4, core: 2. Of those that a mesh axis runs over, the one named last changes fastest.
Arguments:
- raw_integrals: float32 [16, 1024, 512], P(None, 'blk'), may hold values from -0.6 to 0.6
- virtual_coeffs: float32 [512, 256], P(None, 'rep'), may hold values from -0.25 to 0.25
- metric_root: float32 [1024, 1024], P(None, 'rep'), may hold values from -1 to 3, as said below
- occ_energies: float32 [16], P('blk'), may hold values from -2 to -0.5
- virt_energies: float32 [256], replicated, may hold values from 0.2 to 3
Outputs:
- gamma: float32 [16, 256, 1024], P('blk', None, 'rep')
Inputs may be any that keep to these rules, and one draw needn't show every extreme that they name: metric_root is exactly symmetric.
All inputs are finite; a program needn't handle non-finite values.
Results may differ from a plain program's by a relative error of at most 0.0001.
Values sent between devices are 32-bit elements; how exact they have to be, the bound alone decides.
No kernel may reach another device: no remote copies, remote signals or barrier semaphores. Data moves between devices by JAX's collectives and lax.ppermute only.
A program may use at most 64 MiB of HBM per device.

v0:
```python
import jax
import jax.numpy as jnp
from jax import lax
from jax.sharding import PartitionSpec as P

TURNS = 2


def from_behind(x, axis, by):
    count = lax.axis_size(axis)
    return lax.ppermute(x, axis, [(i, (i + by) % count) for i in range(count)])


def pair_terms(own_rows, own_eps, other_rows, other_eps, virt_energies, gradient):
    highest = lax.Precision.HIGHEST
    coulomb = jnp.einsum("xaq,ybq->xyab", own_rows, other_rows, precision=highest)
    spread = virt_energies[:, None] + virt_energies[None, :]
    denominator = spread[None, None] - own_eps[:, None, None, None] - other_eps[None, :, None, None]
    amplitude = (2.0 * coulomb - jnp.swapaxes(coulomb, 2, 3)) / denominator
    return gradient + jnp.einsum("xyab,ybq->xaq", amplitude, other_rows, precision=highest)


def per_device(raw_integrals, virtual_coeffs, metric_root, occ_energies, virt_energies):
    highest = lax.Precision.HIGHEST
    halfway = jnp.einsum("ipm,ma->ipa", raw_integrals, virtual_coeffs, precision=highest)
    regrouped = lax.all_to_all(halfway, "blk", split_axis=0, concat_axis=1, tiled=True)
    complete = lax.all_gather(regrouped, "rep", axis=2, tiled=True)
    fitted_part = jnp.einsum("xpa,pq->xaq", complete, metric_root, precision=highest)
    fitted = lax.all_gather(fitted_part, "rep", axis=2, tiled=True)
    replica = lax.axis_index("rep")
    replicas = lax.axis_size("rep")
    turns = TURNS
    turn_unit = 1
    travel_rows = fitted
    travel_eps = occ_energies
    for bit_index in range((replicas - 1).bit_length()):
        shifted_rows, shifted_eps = from_behind(
            (travel_rows, travel_eps), "blk", (1 << bit_index) * turns
        )
        chosen = replica >> bit_index & 1 == 1
        travel_rows = jnp.where(chosen, shifted_rows, travel_rows)
        travel_eps = jnp.where(chosen, shifted_eps, travel_eps)
    gradient = jnp.zeros(fitted.shape, jnp.float32)

    def advance(turn_index, state_now):
        other_rows, other_eps, total = state_now
        total = pair_terms(fitted, occ_energies, other_rows, other_eps, virt_energies, total)
        other_rows, other_eps = from_behind((other_rows, other_eps), "blk", turn_unit)
        return (other_rows, other_eps, total)

    travel_rows, travel_eps, gradient = lax.fori_loop(
        0, turns - 1, advance, (travel_rows, travel_eps, gradient)
    )
    gradient = pair_terms(fitted, occ_energies, travel_rows, travel_eps, virt_energies, gradient)
    return lax.psum_scatter(gradient, "rep", scatter_dimension=2, tiled=True)


def solution(mesh):
    return jax.shard_map(
        per_device,
        mesh=mesh,
        in_specs=(P(None, "blk", None), P(None, "rep"), P(None, "rep"), P("blk"), P()),
        out_specs=P("blk", None, "rep"),
        check_vma=False,
    )
```

profile of v0, /device:TPU:0, one launch (start us, length us, event | category | flops | bytes accessed | tf_op | source)
XLA Modules:
  0.0 165.9 jit_solution(520824804438171857)
XLA Ops:
  6.5 1.6 copy-done
  8.1 2.7 %fusion.18 = f32[16,64,128]{2,1,0:T(8,128)S(1)} fusion(f32[16,64,512]{2,1,0:T(8,128)S(1)} %copy-done, f32[512,128]{1,0:T(8,128)} %param.6), kind=kOutput, calls=%fused_computation.20 | convolution fusion | flops 805306368 | bytes 2883584 | tf_op jit(solution)/shard_map/ipm,ma->ipa/dot_general | solution.py:25
  10.9 21.6 %all_to_all.12 = f32[16,64,128]{2,1,0:T(8,128)} all-to-all(f32[16,64,128]{2,1,0:T(8,128)S(1)} %fusion.18), channel_id=1, replica_groups=mesh['blk'=16,'rep'=2] {'blk'}, dimensions={0} | all-to-all | bytes 1048576 | tf_op jit(solution)/shard_map/all_to_all | solution.py:26
  32.5 0.0 all-gather.4.cloned.1.call-update
  32.5 0.0 all-gather.6.cloned.1.call-start
  32.5 20.9 %all-gather.4.cloned.1.call-done = f32[1,1024,256]{2,1,0:T(8,128)} async-done(((f32[1,1024,128]{2,1,0:T(8,128)}), f32[1,1024,256]{2,1,0:T(8,128)}) %all-gather.4.cloned.1.call-update) | async-done | bytes 1048592 | tf_op jit(solution)/shard_map/all_gather | solution.py:27
  53.4 4.6 %fusion.8 = f32[256,512]{1,0:T(8,128)} fusion(f32[1024,512]{1,0:T(8,128)} %param.7, f32[1,1024,256]{2,1,0:T(8,128)} %all-gather.4.cloned.1.call-done), kind=kOutput, calls=%fused_computation.9 | convolution fusion | flops 1610612736 | bytes 3670016 | tf_op jit(solution)/shard_map/xpa,pq->xaq/dot_general | solution.py:28
  58.0 0.0 all-gather.6.cloned.1.call-update
  58.1 0.0 reduce-scatter.2.cloned.1.call-start
  58.1 21.4 %all-gather.6.cloned.1.call-done = f32[256,1024]{1,0:T(8,128)} async-done(((f32[256,512]{1,0:T(8,128)}), f32[256,1024]{1,0:T(8,128)}) %all-gather.6.cloned.1.call-update) | async-done | bytes 1048592 | tf_op jit(solution)/shard_map/all_gather | solution.py:29
  79.5 1.5 collective-permute-start
  81.0 26.3 %collective-permute-done = f32[1,256,1024]{2,1,0:T(8,128)} collective-permute-done((f32[1,256,1024]{2,1,0:T(8,128)}, f32[1,256,1024]{2,1,0:T(8,128)}, u32[]{:S(2)}, u32[]{:S(2)}) %collective-permute-start) | collective-permute-done | bytes 1048608 | tf_op jit(solution)/shard_map/ppermute | solution.py:11
  107.3 2.4 %broadcast_select_fusion = f32[1,256,1024]{2,1,0:T(8,128)} fusion(f32[1,256,1024]{2,1,0:T(8,128)} %collective-permute-done, pred[]{:T(512)} %eq.3, f32[256,1024]{1,0:T(8,128)} %all-gather.6.cloned.1.call-done), kind=kLoop, calls=%fused_computation.11 | loop fusion | flops 262144 | bytes 3145729 | tf_op jit(solution)/shard_map/jit(_where)/select_n | solution.py:41
  110.3 5.7 %collective-permute-done.1 = f32[1]{0:T(128)} collective-permute-done((f32[1]{0:T(128)}, f32[1]{0:T(128)}, u32[]{:S(2)}, u32[]{:S(2)}) %collective-permute-start.1) | collective-permute-done | bytes 36 | tf_op jit(solution)/shard_map/ppermute | solution.py:11
  116.7 11.9 %collective-permute-start.3 = (f32[1]{0:T(128)}, f32[1]{0:T(128)}, u32[]{:S(2)}, u32[]{:S(2)}) collective-permute-start(f32[1]{0:T(128)} %select_n.19), channel_id=1, source_target_pairs={{0,2},{2,4},{4,6},{6,8},{8,10},{10,12},{12,14},{14,16},{16,18},{18... | collective-permute-start | bytes 20 | tf_op jit(solution)/shard_map/while/body/eval_jaxpr/ppermute | solution.py:11
  128.6 2.3 %fusion.6 = f32[256,256]{1,0:T(8,128)S(1)} fusion(f32[256,1024]{1,0:T(8,128)S(1)} %copy-done.1, f32[1,256,1024]{2,1,0:T(8,128)} %broadcast_select_fusion), kind=kOutput, calls=%fused_computation.7 | convolution fusion | flops 805306368 | bytes 2359296 | tf_op jit(solution)/shard_map/while/body/eval_jaxpr/xaq,ybq->xyab/dot_general | solution.py:16
  130.8 0.0 copy-start.3
  130.9 0.9 copy.6
  131.7 3.0 %fusion.3 = f32[256,256]{1,0:T(8,128)} fusion(f32[256,1024]{1,0:T(8,128)S(1)} %copy-done.1, f32[1,256,1024]{2,1,0:T(8,128)} %collective-permute-done.2), kind=kOutput, calls=%fused_computation.4 | convolution fusion | flops 805306368 | bytes 2359296 | tf_op jit(solution)/shard_map/xaq,ybq->xyab/dot_general | solution.py:16
  134.7 1.1 copy.8
  135.8 3.1 %fusion.1 = f32[256,1024]{1,0:T(8,128)S(1)} fusion(f32[1,256,1024]{2,1,0:T(8,128)} %collective-permute-done.2, f32[256,256]{1,0:T(8,128)} %fusion.3, f32[256,256]{0,1:T(8,128)S(1)} %copy.8, f32[]{:T(128)} %bitcast.17, f32[]{:T(128)} %bitcast.66, f32[256]{0:T(256)S(1)} %copy-done.3), kind=kOutput, calls=%fused_computation.2 | convolution fusion | flops 805699584 | bytes 2622472 | tf_op jit(solution)/shard_map/xyab,ybq->xaq/dot_general | solution.py:20
  138.9 3.3 %fusion = f32[1,256,1024]{2,1,0:T(8,128)} fusion(f32[256,1024]{1,0:T(8,128)S(1)} %fusion.1, f32[1,256,1024]{2,1,0:T(8,128)} %broadcast_select_fusion, f32[256,256]{1,0:T(8,128)S(1)} %fusion.6, f32[256,256]{0,1:T(8,128)S(1)} %copy-done.2, f32[]{:T(128)} %bitcast.11, f32[]{:T(128)} %bitcast.65, f32[256]{0:T(256)S(1)} %copy-done.3), kind=kOutput, calls=%fused_computation.1 | convolution fusion | flops 805961728 | bytes 3671048 | tf_op jit(solution)/shard_map/while/body/eval_jaxpr/xyab,ybq->xaq/dot_general | solution.py:20
  142.2 0.0 reduce-scatter.2.cloned.1.call-update
  142.3 17.1 %reduce-scatter.2.cloned.1.call-done = f32[1,256,512]{2,1,0:T(8,128)} async-done(((f32[1,256,1024]{2,1,0:T(8,128)}), f32[1,256,512]{2,1,0:T(8,128)}) %reduce-scatter.2.cloned.1.call-update) | async-done | bytes 524304 | tf_op jit(solution)/shard_map/reduce_scatter | solution.py:55
  (11 shorter events, 0.0 us)
Async XLA Ops:
  6.5 1.6 copy-start
  6.5 46.9 %all-gather.4.cloned.1.call-start = ((), (), s32[]{:S(2)}) async-start(), calls=%async_computation.2 | async-start | bytes 1572864 | tf_op jit(solution)/shard_map/all_gather | solution.py:27
  32.5 47.0 %all-gather.6.cloned.1.call-start = ((), (), s32[]{:S(2)}) async-start(), calls=%async_computation.4 | async-start | bytes 1572864 | tf_op jit(solution)/shard_map/all_gather | solution.py:29
  58.1 101.3 %reduce-scatter.2.cloned.1.call-start = ((), (), s32[]{:S(2)}) async-start(), calls=%async_computation.3 | async-start | bytes 1572864 | tf_op jit(solution)/shard_map/reduce_scatter | solution.py:55
  79.5 49.1 %copy-start.1 = (f32[256,1024]{1,0:T(8,128)S(1)}, f32[256,1024]{1,0:T(8,128)}, u32[]{:S(2)}) copy-start(f32[256,1024]{1,0:T(8,128)} %all-gather.6.cloned.1.call-done) | copy-start | bytes 3145732
  79.5 27.7 %collective-permute-start = (f32[1,256,1024]{2,1,0:T(8,128)}, f32[1,256,1024]{2,1,0:T(8,128)}, u32[]{:S(2)}, u32[]{:S(2)}) collective-permute-start(f32[1,256,1024]{2,1,0:T(8,128)} %bitcast.67), channel_id=1, source_target_pairs={{0,4},{2,6},{4,8},{6,10},{8,12},{10,14},{12,16},{14,18},{16,20},{1... | collective-permute-start | bytes 3145736 | tf_op jit(solution)/shard_map/ppermute | solution.py:11
  109.7 22.1 %collective-permute-start.2 = (f32[1,256,1024]{2,1,0:T(8,128)}, f32[1,256,1024]{2,1,0:T(8,128)}, u32[]{:S(2)}, u32[]{:S(2)}) collective-permute-start(f32[1,256,1024]{2,1,0:T(8,128)} %broadcast_select_fusion), channel_id=1, source_target_pairs={{0,2},{2,4},{4,6},{6,8},{8,10},{10,12},{12,14},{14,16},{16,18},{18... | collective-permute-start | bytes 3145736 | tf_op jit(solution)/shard_map/while/body/eval_jaxpr/ppermute | solution.py:11
  109.7 6.4 %collective-permute-start.1 = (f32[1]{0:T(128)}, f32[1]{0:T(128)}, u32[]{:S(2)}, u32[]{:S(2)}) collective-permute-start(f32[1]{0:T(128)} %param.8), channel_id=1, source_target_pairs={{0,4},{2,6},{4,8},{6,10},{8,12},{10,14},{12,16},{14,18},{16,20},{1... | collective-permute-start | bytes 20 | tf_op jit(solution)/shard_map/ppermute | solution.py:11
  116.7 19.1 %collective-permute-start.3 = (f32[1]{0:T(128)}, f32[1]{0:T(128)}, u32[]{:S(2)}, u32[]{:S(2)}) collective-permute-start(f32[1]{0:T(128)} %select_n.19), channel_id=1, source_target_pairs={{0,2},{2,4},{4,6},{6,8},{8,10},{10,12},{12,14},{14,16},{16,18},{18... | collective-permute-start | bytes 20 | tf_op jit(solution)/shard_map/while/body/eval_jaxpr/ppermute | solution.py:11
  130.8 5.0 %copy-start.3 = (f32[256]{0:T(256)S(1)}, f32[256]{0:T(256)}, u32[]{:S(2)}) copy-start(f32[256]{0:T(256)} %param.9) | copy-start | bytes 3076
  134.7 4.2 %copy-start.2 = (f32[256,256]{0,1:T(8,128)S(1)}, f32[256,256]{0,1:T(8,128)}, u32[]{:S(2)}) copy-start(f32[256,256]{0,1:T(8,128)} %copy.6) | copy-start | bytes 786436
Sparse Core Ops, SparseCore 0:
  32.6 20.7 all-gather.3
  58.2 21.2 all-gather.5
  142.4 16.9 reduce-scatter.1
where the time goes:
time: 166 us
  waiting for transfers between devices  91.4 us (55%)
  blocking collectives  21.6 us (13%)
  matrix products  19 us (11%)
  between operations  14.6 us (9%)
  starting transfers between devices  13.4 us (8%)
  local copies, waits for them, and re-layouts  3.58 us (2%)
  other arithmetic  2.4 us (1%)
    ppermute x4, waiting for transfers between devices, from_behind(): return lax.ppermute(x, axis, [(i, (i + by) % count) for i in range(count)])  31.9 us
    all_to_all x1, blocking collectives, per_device(): lax.all_to_all(halfway, 'blk', split_axis=0, concat_axis=1, tiled=True)  21.6 us
    all_gather x1, waiting for transfers between devices, per_device(): fitted = lax.all_gather(fitted_part, 'rep', axis=2, tiled=True)  21.4 us
    all_gather x1, waiting for transfers between devices, per_device(): complete = lax.all_gather(regrouped, 'rep', axis=2, tiled=True)  20.9 us
    reduce_scatter x1, waiting for transfers between devices, per_device(): return lax.psum_scatter(gradient, 'rep', scatter_dimension=2, tiled=True)  17.1 us
    ppermute x4, starting transfers between devices, from_behind(): return lax.ppermute(x, axis, [(i, (i + by) % count) for i in range(count)])  13.3 us
    dot_general x2, matrix products, pair_terms(): jnp.einsum('xyab,ybq->xaq', amplitude, other_rows, precision=highest)  6.38 us
    dot_general x2, matrix products, pair_terms(): jnp.einsum('xaq,ybq->xyab', own_rows, other_rows, precision=highest)  5.22 us
  transfers between devices with their start and end apart: 7, of which 5 were waited for; matrix products, arithmetic and copies ran while one was open for 4% of the time, Pallas kernels for 0%

commit v1 on v0

--- a/solution.py
+++ b/solution.py
@@ -26,7 +26,14 @@
     regrouped = lax.all_to_all(halfway, "blk", split_axis=0, concat_axis=1, tiled=True)
     complete = lax.all_gather(regrouped, "rep", axis=2, tiled=True)
     fitted_part = jnp.einsum("xpa,pq->xaq", complete, metric_root, precision=highest)
-    fitted = lax.all_gather(fitted_part, "rep", axis=2, tiled=True)
+    ways, here, lap = (lax.axis_size("rep"), lax.axis_index("rep"), fitted_part.shape[2])
+    line, have = (fitted_part, 1)
+    while have < ways:
+        line = jnp.concatenate(
+            [line, lax.ppermute(line, "rep", [(d, (d - have) % ways) for d in range(ways)])], axis=2
+        )
+        have = 2 * have
+    fitted = jnp.roll(line, here * lap, axis=2)
     replica = lax.axis_index("rep")
     replicas = lax.axis_size("rep")
     turns = TURNS

time: 166 us -> 158 us (0.952)
  waiting for transfers between devices: 91.4 us -> 83.1 us
    all_gather x1 -> x0, waiting for transfers between devices: 21.4 us -> none  [per_device(): fitted = lax.all_gather(fitted_part, 'rep', axis=2, tiled=True)]
    ppermute x0 -> x1, waiting for transfers between devices: none -> 12.9 us  [per_device(): lax.ppermute(line, 'rep', [(d, (d - have) % ways) for d in range(ways)])]
  transfers between devices with their start and end apart: 7 -> 7, of which waited for: 5 -> 5; matrix products, arithmetic and copies ran while one was open for 4% -> 5% of each run, Pallas kernels for 0% -> 0%
where the time goes in v1:
time: 158 us
  waiting for transfers between devices  83.1 us (53%)
  blocking collectives  21.6 us (14%)
  matrix products  18.2 us (12%)
  between operations  14.7 us (9%)
  starting transfers between devices  13.7 us (9%)
  local copies, waits for them, and re-layouts  3.91 us (2%)
  other arithmetic  2.71 us (2%)
    ppermute x4, waiting for transfers between devices, from_behind(): return lax.ppermute(x, axis, [(i, (i + by) % count) for i in range(count)])  31 us
    all_to_all x1, blocking collectives, per_device(): lax.all_to_all(halfway, 'blk', split_axis=0, concat_axis=1, tiled=True)  21.6 us
    all_gather x1, waiting for transfers between devices, per_device(): complete = lax.all_gather(regrouped, 'rep', axis=2, tiled=True)  20.9 us
    reduce_scatter x1, waiting for transfers between devices, per_device(): return lax.psum_scatter(gradient, 'rep', scatter_dimension=2, tiled=True)  18.2 us
    ppermute x4, starting transfers between devices, from_behind(): return lax.ppermute(x, axis, [(i, (i + by) % count) for i in range(count)])  13.2 us
    ppermute x1, waiting for transfers between devices, per_device(): lax.ppermute(line, 'rep', [(d, (d - have) % ways) for d in range(ways)])  12.9 us
    dot_general x2, matrix products, pair_terms(): jnp.einsum('xyab,ybq->xaq', amplitude, other_rows, precision=highest)  6.38 us
    dot_general x2, matrix products, pair_terms(): jnp.einsum('xaq,ybq->xyab', own_rows, other_rows, precision=highest)  5.22 us
  transfers between devices with their start and end apart: 7, of which 5 were waited for; matrix products, arithmetic and copies ran while one was open for 5% of the time, Pallas kernels for 0%

profile of v1, /device:TPU:0, one launch (start us, length us, event | category | flops | bytes accessed | tf_op | source)
XLA Modules:
  0.0 157.9 jit_solution(7391851413034033390)
XLA Ops:
  6.5 1.6 %copy-done = f32[16,64,512]{2,1,0:T(8,128)S(1)} copy-done((f32[16,64,512]{2,1,0:T(8,128)S(1)}, f32[16,64,512]{2,1,0:T(8,128)}, u32[]{:S(2)}) %copy-start) | copy-done | bytes 2097176
  8.1 2.7 %fusion.22 = f32[16,64,128]{2,1,0:T(8,128)S(1)} fusion(f32[16,64,512]{2,1,0:T(8,128)S(1)} %copy-done, f32[512,128]{1,0:T(8,128)} %param.6), kind=kOutput, calls=%fused_computation.29 | convolution fusion | flops 805306368 | bytes 2883584 | tf_op jit(solution)/shard_map/ipm,ma->ipa/dot_general | solution.py:25
  10.9 21.6 %all_to_all.12 = f32[16,64,128]{2,1,0:T(8,128)} all-to-all(f32[16,64,128]{2,1,0:T(8,128)S(1)} %fusion.22), channel_id=1, replica_groups=mesh['blk'=16,'rep'=2] {'blk'}, dimensions={0} | all-to-all | bytes 1048576 | tf_op jit(solution)/shard_map/all_to_all | solution.py:26
  32.5 0.0 all-gather.2.cloned.1.call-update
  32.5 0.0 reduce-scatter.2.cloned.1.call-start
  32.5 20.9 %all-gather.2.cloned.1.call-done = f32[1,1024,256]{2,1,0:T(8,128)} async-done(((f32[1,1024,128]{2,1,0:T(8,128)}), f32[1,1024,256]{2,1,0:T(8,128)}) %all-gather.2.cloned.1.call-update) | async-done | bytes 1048592 | tf_op jit(solution)/shard_map/all_gather | solution.py:27
  53.4 3.8 %convolution_bitcast_fusion = f32[1,256,512]{2,1,0:T(8,128)S(1)} fusion(f32[1024,512]{1,0:T(8,128)} %param.7, f32[1,1024,256]{2,1,0:T(8,128)} %all-gather.2.cloned.1.call-done), kind=kOutput, calls=%fused_computation.6 | convolution fusion | flops 1610612736 | bytes 3670016 | tf_op jit(solution)/shard_map/xpa,pq->xaq/dot_general | solution.py:28
  57.3 0.4 collective-permute-start
  57.7 0.4 copy-done.1
  58.1 12.9 %collective-permute-done = f32[1,256,512]{2,1,0:T(8,128)} collective-permute-done((f32[1,256,512]{2,1,0:T(8,128)S(1)}, f32[1,256,512]{2,1,0:T(8,128)}, u32[]{:S(2)}, u32[]{:S(2)}) %collective-permute-start) | collective-permute-done | bytes 524320 | tf_op jit(solution)/shard_map/ppermute | solution.py:33
  70.9 1.6 %fusion.3 = f32[1,256,1024]{2,1,0:T(8,128)S(1)} fusion(s32[]{:T(128)S(6)} %select_n.31, f32[1,256,512]{2,1,0:T(8,128)} %copy-done.1, f32[1,256,512]{2,1,0:T(8,128)} %collective-permute-done), kind=kLoop, calls=%fused_computation.9 | loop fusion | flops 786432 | bytes 2097156 | tf_op jit(solution)/shard_map/jit(_roll_dynamic)/concatenate | solution.py:36
  72.5 1.5 collective-permute-start.1
  74.1 25.2 %collective-permute-done.1 = f32[1,256,1024]{2,1,0:T(8,128)} collective-permute-done((f32[1,256,1024]{2,1,0:T(8,128)S(1)}, f32[1,256,1024]{2,1,0:T(8,128)}, u32[]{:S(2)}, u32[]{:S(2)}) %collective-permute-start.1) | collective-permute-done | bytes 1048608 | tf_op jit(solution)/shard_map/ppermute | solution.py:11
  99.3 1.1 broadcast_select_fusion
  101.1 5.8 %collective-permute-done.2 = f32[1]{0:T(128)} collective-permute-done((f32[1]{0:T(128)}, f32[1]{0:T(128)}, u32[]{:S(2)}, u32[]{:S(2)}) %collective-permute-start.2) | collective-permute-done | bytes 36 | tf_op jit(solution)/shard_map/ppermute | solution.py:11
  107.5 11.7 %collective-permute-start.4 = (f32[1]{0:T(128)}, f32[1]{0:T(128)}, u32[]{:S(2)}, u32[]{:S(2)}) collective-permute-start(f32[1]{0:T(128)} %select_n.34), channel_id=1, source_target_pairs={{0,2},{2,4},{4,6},{6,8},{8,10},{10,12},{12,14},{14,16},{16,18},{18... | collective-permute-start | bytes 20 | tf_op jit(solution)/shard_map/while/body/eval_jaxpr/ppermute | solution.py:11
  119.2 2.3 %fusion.9 = f32[256,256]{1,0:T(8,128)S(1)} fusion(f32[1,256,1024]{2,1,0:T(8,128)S(1)} %fusion.3, f32[1,256,1024]{2,1,0:T(8,128)} %broadcast_select_fusion), kind=kOutput, calls=%fused_computation.15 | convolution fusion | flops 805306368 | bytes 2359296 | tf_op jit(solution)/shard_map/while/body/eval_jaxpr/xaq,ybq->xyab/dot_general | solution.py:16
  121.4 0.8 copy.6
  122.3 3.0 %fusion.6 = f32[256,256]{1,0:T(8,128)} fusion(f32[1,256,1024]{2,1,0:T(8,128)} %collective-permute-done.3, f32[1,256,1024]{2,1,0:T(8,128)S(1)} %fusion.3), kind=kOutput, calls=%fused_computation.12 | convolution fusion | flops 805306368 | bytes 2359296 | tf_op jit(solution)/shard_map/xaq,ybq->xyab/dot_general | solution.py:16
  125.2 1.1 copy.8
  126.4 3.1 %fusion.4 = f32[256,1024]{1,0:T(8,128)S(1)} fusion(f32[1,256,1024]{2,1,0:T(8,128)} %collective-permute-done.3, f32[256,256]{1,0:T(8,128)} %fusion.6, f32[256,256]{0,1:T(8,128)S(1)} %copy.8, f32[]{:T(128)} %bitcast.18, f32[]{:T(128)} %bitcast.69, f32[256]{0:T(256)S(1)} %copy-done.3), kind=kOutput, calls=%fused_computation.10 | convolution fusion | flops 805699584 | bytes 2622472 | tf_op jit(solution)/shard_map/xyab,ybq->xaq/dot_general | solution.py:20
  129.5 3.3 %fusion = f32[1,256,1024]{2,1,0:T(8,128)} fusion(f32[256,1024]{1,0:T(8,128)S(1)} %fusion.4, f32[1,256,1024]{2,1,0:T(8,128)} %broadcast_select_fusion, f32[256,256]{1,0:T(8,128)S(1)} %fusion.9, f32[256,256]{0,1:T(8,128)S(1)} %copy-done.2, f32[]{:T(128)} %bitcast.12, f32[]{:T(128)} %bitcast.68, f32[256]{0:T(256)S(1)} %copy-done.3), kind=kOutput, calls=%fused_computation.5 | convolution fusion | flops 805961728 | bytes 3671048 | tf_op jit(solution)/shard_map/while/body/eval_jaxpr/xyab,ybq->xaq/dot_general | solution.py:20
  132.8 0.0 reduce-scatter.2.cloned.1.call-update
  132.8 18.2 %reduce-scatter.2.cloned.1.call-done = f32[1,256,512]{2,1,0:T(8,128)} async-done(((f32[1,256,1024]{2,1,0:T(8,128)}), f32[1,256,512]{2,1,0:T(8,128)}) %reduce-scatter.2.cloned.1.call-update) | async-done | bytes 524304 | tf_op jit(solution)/shard_map/reduce_scatter | solution.py:62
  (11 shorter events, 0.0 us)
Async XLA Ops:
  6.5 1.6 %copy-start = (f32[16,64,512]{2,1,0:T(8,128)S(1)}, f32[16,64,512]{2,1,0:T(8,128)}, u32[]{:S(2)}) copy-start(f32[16,64,512]{2,1,0:T(8,128)} %param.5) | copy-start | bytes 6291460
  6.5 46.9 %all-gather.2.cloned.1.call-start = ((), (), s32[]{:S(2)}) async-start(), calls=%async_computation.2 | async-start | bytes 1572864 | tf_op jit(solution)/shard_map/all_gather | solution.py:27
  32.5 118.6 %reduce-scatter.2.cloned.1.call-start = ((), (), s32[]{:S(2)}) async-start(), calls=%async_computation.3 | async-start | bytes 1572864 | tf_op jit(solution)/shard_map/reduce_scatter | solution.py:62
  57.3 0.8 copy-start.1
  57.3 13.7 %collective-permute-start = (f32[1,256,512]{2,1,0:T(8,128)S(1)}, f32[1,256,512]{2,1,0:T(8,128)}, u32[]{:S(2)}, u32[]{:S(2)}) collective-permute-start(f32[1,256,512]{2,1,0:T(8,128)S(1)} %convolution_bitcast_fusion), channel_id=1, source_target_pairs={{0,1},{1,0},{2,3},{3,2},{4,5},{5,4},{6,7},{7,6},{8,9},{9,8},{10,11... | collective-permute-start | bytes 1572872 | tf_op jit(solution)/shard_map/ppermute | solution.py:33
  72.5 26.7 %collective-permute-start.1 = (f32[1,256,1024]{2,1,0:T(8,128)S(1)}, f32[1,256,1024]{2,1,0:T(8,128)}, u32[]{:S(2)}, u32[]{:S(2)}) collective-permute-start(f32[1,256,1024]{2,1,0:T(8,128)S(1)} %fusion.3), channel_id=1, source_target_pairs={{0,4},{2,6},{4,8},{6,10},{8,12},{10,14},{12,16},{14,18},{16,20},{1... | collective-permute-start | bytes 3145736 | tf_op jit(solution)/shard_map/ppermute | solution.py:11
  100.4 21.9 %collective-permute-start.3 = (f32[1,256,1024]{2,1,0:T(8,128)}, f32[1,256,1024]{2,1,0:T(8,128)}, u32[]{:S(2)}, u32[]{:S(2)}) collective-permute-start(f32[1,256,1024]{2,1,0:T(8,128)} %broadcast_select_fusion), channel_id=1, source_target_pairs={{0,2},{2,4},{4,6},{6,8},{8,10},{10,12},{12,14},{14,16},{16,18},{18... | collective-permute-start | bytes 3145736 | tf_op jit(solution)/shard_map/while/body/eval_jaxpr/ppermute | solution.py:11
  100.4 6.5 %collective-permute-start.2 = (f32[1]{0:T(128)}, f32[1]{0:T(128)}, u32[]{:S(2)}, u32[]{:S(2)}) collective-permute-start(f32[1]{0:T(128)} %param.8), channel_id=1, source_target_pairs={{0,4},{2,6},{4,8},{6,10},{8,12},{10,14},{12,16},{14,18},{16,20},{1... | collective-permute-start | bytes 20 | tf_op jit(solution)/shard_map/ppermute | solution.py:11
  107.5 18.9 %collective-permute-start.4 = (f32[1]{0:T(128)}, f32[1]{0:T(128)}, u32[]{:S(2)}, u32[]{:S(2)}) collective-permute-start(f32[1]{0:T(128)} %select_n.34), channel_id=1, source_target_pairs={{0,2},{2,4},{4,6},{6,8},{8,10},{10,12},{12,14},{14,16},{16,18},{18... | collective-permute-start | bytes 20 | tf_op jit(solution)/shard_map/while/body/eval_jaxpr/ppermute | solution.py:11
  121.4 4.9 %copy-start.3 = (f32[256]{0:T(256)S(1)}, f32[256]{0:T(256)}, u32[]{:S(2)}) copy-start(f32[256]{0:T(256)} %param.9) | copy-start | bytes 3076
  125.2 4.2 %copy-start.2 = (f32[256,256]{0,1:T(8,128)S(1)}, f32[256,256]{0,1:T(8,128)}, u32[]{:S(2)}) copy-start(f32[256,256]{0,1:T(8,128)} %copy.6) | copy-start | bytes 786436
Sparse Core Ops, SparseCore 0:
  32.6 20.7 all-gather.1
  132.9 18.0 reduce-scatter.1
